TPU v7x, 32 devices: a whole 2x2x4 slice. The times are simulated.
32 devices in a mesh: seq: 16 (over z, y, core), fsdp: 2 (over x).
Axes of the slice: x: 2, y: 2, z: 4, core: 2. Of those that a mesh axis runs over, the one named last changes fastest.
Arguments:
- residual: bfloat16 [2, 1024, 1440], P('fsdp', 'seq'), may hold values from -40 to 40
- queries: bfloat16 [2, 1024, 2048], P('fsdp', 'seq'), may hold values from -64 to 64
- key_rows: bfloat16 [2, 1024, 256], P('fsdp', 'seq'), may hold values from -16 to 16
- values: bfloat16 [2, 1024, 256], P('fsdp', 'seq'), may hold values from -1 to 2
- attention_sinks: float32 [32], replicated, may hold values from 0 to 6
- out_weight: bfloat16 [2048, 1440], P('seq', 'fsdp'), may hold values from -0.125 to 0.125
- norm_gain: bfloat16 [1440], replicated, may hold values from 0.25 to 1.75
- router_weight: bfloat16 [1440, 16], replicated, may hold values from -0.15625 to 0.15625
- gate_weight: bfloat16 [1440, 23040], P(None, 'seq'), may hold values from -0.15625 to 0.15625
- up_weight: bfloat16 [1440, 23040], P(None, 'seq'), may hold values from -0.15625 to 0.15625
- down_weight: bfloat16 [23040, 1440], P('seq'), may hold values from -0.15625 to 0.15625
- routing: int32 [2, 1024, 2], P('fsdp', 'seq'), may hold values from 0 to 15, as said below
- span_order: int32 [32], replicated, may hold values from 0 to 31, as said below
Outputs:
- attended: bfloat16 [2, 1024, 1440], P('fsdp', 'seq')
- layer_output: bfloat16 [2, 1024, 1440], P('fsdp', 'seq')
Inputs may be any that keep to these rules, and one draw needn't show every extreme that they name: A permutation of 0 to 31; index i of seq holds the rows of spans span_order[2 i] and span_order[2 i + 1], and these two add up to 31. `routing`: in the rows of one device no expert is named more than 12 times; in each prompt one expert is named exactly 12 times in the rows of every device; the 2 experts of a row differ.
All inputs are finite; a program needn't handle non-finite values.
Results may differ from a plain program's by a relative error of at most 0.009.
Values may be sent and summed in bfloat16 or wider, within the bound.
A program may use at most 64 MiB of HBM per device.

v0:
```python
import jax
import jax.numpy as jnp
from jax import lax
from jax.sharding import PartitionSpec as P

D = 1440
HEADS = 32
KVH = 4
HD = 64
EXPERTS = 16
TOPK = 2
TOK_DEV = 64
HALF = 32
CAP = 12


rope_base = 150000.0
norm_eps = 1e-05
masked_score = -1e30
block_rows = 512


def lookup(table_values, lookup_index):
    matches = lookup_index[:, None] == jnp.arange(table_values.shape[0], dtype=jnp.int32)[None, :]
    return jnp.sum(jnp.where(matches, table_values[None, :], 0), axis=1)


def positions(span_order, row_index):
    device = row_index // TOK_DEV
    within = row_index % TOK_DEV
    span_index = lookup(span_order, 2 * device + within // HALF)
    return span_index * HALF + within % HALF


def rotate(head_values, where_at):
    half_size = head_values.shape[-1] // 2
    frequency = jnp.exp(-jnp.log(rope_base) * jnp.arange(half_size, dtype=jnp.float32) / half_size)
    angles = where_at.astype(jnp.float32)[:, None] * frequency[None, :]
    cosine = jnp.cos(angles)[:, None, :]
    sine_part = jnp.sin(angles)[:, None, :]
    first_half = head_values[..., :half_size]
    second = head_values[..., half_size:]
    return jnp.concatenate(
        [first_half * cosine - second * sine_part, second * cosine + first_half * sine_part],
        axis=-1,
    )


def slot_of(chosen):
    flattened = chosen.reshape(-1)
    onehot = (flattened[:, None] == jnp.arange(EXPERTS, dtype=jnp.int32)[None, :]).astype(jnp.int32)
    before = jnp.cumsum(onehot, axis=0) - onehot
    return jnp.sum(before * onehot, axis=1).reshape(chosen.shape)


def expert_block(flattened, gate_weight, up_weight, down_weight):
    gate_values = jnp.dot(flattened, gate_weight, preferred_element_type=jnp.float32)
    up_values = jnp.dot(flattened, up_weight, preferred_element_type=jnp.float32)
    hidden = (gate_values * jax.nn.sigmoid(1.702 * gate_values) * (up_values + 1.0)).astype(
        jnp.bfloat16
    )
    return jnp.dot(hidden, down_weight, preferred_element_type=jnp.float32).astype(jnp.bfloat16)


def on_device(
    residual,
    queries,
    key_rows,
    values,
    attention_sinks,
    out_weight,
    norm_gain,
    router_weight,
    gate_weight,
    up_weight,
    down_weight,
    routing,
    span_order,
):
    seq_count = lax.axis_size("seq")
    seq_index = lax.axis_index("seq")
    token_count = residual.shape[1]
    group_size = HEADS // KVH
    score_scale = HD ** (-0.5)
    query_at = positions(
        span_order, seq_index * token_count + jnp.arange(token_count, dtype=jnp.int32)
    )
    query_rot = rotate(
        queries[0].astype(jnp.float32).reshape(token_count, HEADS, HD), query_at
    ).astype(jnp.bfloat16)
    query_rot = query_rot.reshape(token_count, KVH, group_size, HD)
    key_rot = rotate(
        key_rows[0].astype(jnp.float32).reshape(token_count, KVH, HD), query_at
    ).astype(jnp.bfloat16)
    key_rot = key_rot.reshape(token_count, KVH * HD)

    def block_update(carried, key_block, value_block, first_row):
        running_max, running_sum, running_out = carried
        block_size = key_block.shape[0]
        key_at = positions(span_order, first_row + jnp.arange(block_size, dtype=jnp.int32))
        key_heads = key_block.reshape(block_size, KVH, HD)
        value_heads = value_block.reshape(block_size, KVH, HD)
        scores = (
            jnp.einsum("tkgd,rkd->tkgr", query_rot, key_heads, preferred_element_type=jnp.float32)
            * score_scale
        )
        visible = key_at[None, :] <= query_at[:, None]
        scores = jnp.where(visible[:, None, None, :], scores, masked_score)
        new_max = jnp.maximum(running_max, jnp.max(scores, axis=-1))
        rescale = jnp.exp(running_max - new_max)
        weights = jnp.exp(scores - new_max[..., None])
        running_sum = running_sum * rescale + jnp.sum(weights, axis=-1)
        running_out = running_out * rescale[..., None] + jnp.einsum(
            "tkgr,rkd->tkgd",
            weights.astype(jnp.bfloat16),
            value_heads,
            preferred_element_type=jnp.float32,
        )
        return (new_max, running_sum, running_out)

    sink_start = jnp.broadcast_to(
        attention_sinks.reshape(1, KVH, group_size), (token_count, KVH, group_size)
    )
    initial = (
        sink_start,
        jnp.ones((token_count, KVH, group_size), jnp.float32),
        jnp.zeros((token_count, KVH, group_size, HD), jnp.float32),
    )
    carried = initial
    key_piece = lax.all_gather(key_rot, "seq", axis=0, tiled=True)
    value_piece = lax.all_gather(values[0], "seq", axis=0, tiled=True)
    piece_rows = key_piece.shape[0]
    block_size = min(piece_rows, block_rows)
    full_blocks = piece_rows // block_size

    def scan_step(inner_state, offset):
        key_block = lax.dynamic_slice_in_dim(key_piece, offset, block_size, 0)
        value_block = lax.dynamic_slice_in_dim(value_piece, offset, block_size, 0)
        return (block_update(inner_state, key_block, value_block, offset), None)

    carried, unused = lax.scan(
        scan_step, carried, jnp.arange(full_blocks, dtype=jnp.int32) * block_size
    )
    final_max, final_sum, final_out = carried
    attention_rows = (
        (final_out / final_sum[..., None]).reshape(token_count, HEADS * HD).astype(jnp.bfloat16)
    )
    column_rows = lax.all_gather(out_weight, "seq", axis=0, tiled=True)
    projected = jnp.dot(
        lax.all_gather(attention_rows, "fsdp", axis=0, tiled=True),
        column_rows,
        preferred_element_type=jnp.float32,
    ).astype(jnp.bfloat16)
    attended = lax.all_to_all(projected, "fsdp", split_axis=0, concat_axis=1, tiled=True)
    stream = residual[0].astype(jnp.float32) + attended.astype(jnp.float32)
    normed = (
        stream
        * lax.rsqrt(jnp.mean(stream * stream, axis=-1, keepdims=True) + norm_eps)
        * norm_gain.astype(jnp.float32)
    ).astype(jnp.bfloat16)
    logits = jnp.dot(normed, router_weight, preferred_element_type=jnp.float32)
    chosen = routing[0]
    matches = chosen[:, :, None] == jnp.arange(EXPERTS, dtype=jnp.int32)[None, None, :]
    chosen_logits = jnp.sum(jnp.where(matches, logits[:, None, :], 0.0), axis=-1)
    gates = 1.0 / jnp.sum(jnp.exp(chosen_logits[:, :, None] - chosen_logits[:, None, :]), axis=1)
    slot_index = slot_of(chosen)
    target = chosen * CAP + slot_index
    dispatch_map = jnp.sum(
        (target[None, :, :] == jnp.arange(EXPERTS * CAP, dtype=jnp.int32)[:, None, None]).astype(
            jnp.int32
        ),
        axis=2,
    )
    buffer = jnp.dot(
        dispatch_map.astype(jnp.bfloat16), normed, preferred_element_type=jnp.float32
    ).astype(jnp.bfloat16)
    copies = seq_count // EXPERTS
    outgoing = jnp.broadcast_to(
        buffer.reshape(EXPERTS, 1, CAP, D), (EXPERTS, copies, CAP, D)
    ).reshape(seq_count, CAP, D)
    arrived = lax.all_to_all(outgoing, "seq", split_axis=0, concat_axis=0, tiled=True)
    sources = arrived.shape[0]
    slot_count = arrived.shape[1]
    partial_value = expert_block(
        arrived.reshape(sources * slot_count, D), gate_weight, up_weight, down_weight
    )
    returned = lax.all_to_all(
        partial_value.reshape(sources, slot_count, D),
        "seq",
        split_axis=0,
        concat_axis=0,
        tiled=True,
    )
    summed = jnp.sum(returned.reshape(EXPERTS, copies, CAP, D).astype(jnp.float32), axis=1).reshape(
        EXPERTS * CAP, D
    )
    chosen_out = jnp.take(summed, target.reshape(-1), axis=0).reshape(token_count, TOPK, D)
    expert_mix = jnp.sum(chosen_out * gates[:, :, None], axis=1)
    layer_output = (stream + expert_mix).astype(jnp.bfloat16)
    return (attended[None], layer_output[None])


def solution(mesh):
    in_specs = (
        P("fsdp", "seq", None),
        P("fsdp", "seq", None),
        P("fsdp", "seq", None),
        P("fsdp", "seq", None),
        P(),
        P("seq", "fsdp"),
        P(),
        P(),
        P(None, "seq"),
        P(None, "seq"),
        P("seq", None),
        P("fsdp", "seq", None),
        P(),
    )
    out_specs = (P("fsdp", "seq", None), P("fsdp", "seq", None))
    return jax.shard_map(
        on_device, mesh=mesh, in_specs=in_specs, out_specs=out_specs, check_vma=False
    )
```

profile of v0, /device:TPU:0, one launch (start us, length us, event | category | flops | bytes accessed | tf_op | source)
XLA Modules:
  0.0 178.8 jit_solution(1170049440851932638)
XLA Ops:
  7.2 0.7 all-gather.3.cloned.1.call-update
  8.0 0.7 select_reduce_fusion.3
  8.8 1.4 reshape.355
  10.1 1.4 fusion.41
  11.7 0.2 multiply_cosine_fusion
  12.3 25.3 %all_gather.12 = bf16[1024,256]{1,0:T(8,128)(2,1)S(1)} all-gather(bf16[64,256]{1,0:T(8,128)(2,1)S(1)} %convert_element_type.102), channel_id=1, replica_groups=mesh['seq'=16,'fsdp'=2] {'seq'}, dimensions={0}, use_global_device_ids=true | all-gather | bytes 557056 | tf_op jit(solution)/shard_map/all_gather | solution.py:130
  37.7 2.5 %subtract_convert_fusion = (bf16[64,32,32]{2,0,1:T(8,128)(2,1)S(1)}, bf16[64,32,32]{2,0,1:T(8,128)(2,1)S(1)}) fusion(f32[64,32,32]{2,1,0:T(8,128)} %get-tuple-element.258, f32[64,32,32]{2,1,0:T(8,128)S(1)} %get-tuple-element.257, f32[64,32]{1,0:T(8,128)S(1)} %get-tuple-element.264, f32[64,32]{1,0:T(8,128)S(1)} %get-tuple-element.263), kind=kLoop, calls=%fused_computation.53 | loop fusion | flops 524288 | bytes 802816 | tf_op jit(solution)/shard_map/convert.8
  40.1 0.3 pad_maximum_fusion
  40.4 20.8 %all-gather = bf16[1,1024,256]{2,1,0:T(8,128)(2,1)S(1)} all-gather(bf16[1,64,256]{2,1,0:T(8,128)(2,1)S(1)} %copy-done.6), channel_id=2, replica_groups=mesh['seq'=16,'fsdp'=2] {'seq'}, dimensions={1}, use_global_device_ids=true | all-gather | bytes 557056 | tf_op jit(solution)/shard_map/all_gather | solution.py:131
  61.3 24.2 %while.18 = (s32[]{:T(128)}, f32[64,4,8]{0,2,1:T(8,128)S(1)}, f32[64,4,8]{0,2,1:T(8,128)S(1)}, f32[64,4,8,64]{0,3,2,1:T(8,128)S(1)}, s32[2]{0:T(128)S(1)}, /*ind...) while((s32[]{:T(128)}, f32[64,4,8]{0,2,1:T(8,128)S(1)}, ...), condition=%wide.region_5.6_spmd.clone, body=%wide.region_1.5_spmd.clone.sunk | while | flops 280482304 | bytes 33567324 | solution.py:141
  61.3 0.6 dynamic_slice.30
  64.1 0.7 fusion.71
  64.9 0.7 fusion.72
  65.6 0.8 fusion.73
  66.4 1.9 %copy-done.1 = f32[4,512,64,8]{1,2,3,0:T(8,128)} copy-done((f32[4,512,64,8]{1,2,3,0:T(8,128)}, f32[4,512,64,8]{1,2,3,0:T(8,128)S(1)}, u32[]{:S(2)}) %copy-start.1) | copy-done | bytes 4194328 | tf_op jit(solution)/shard_map/while
  68.4 1.3 fusion.74
  69.8 3.6 %fusion.76 = f32[64,4,8,64]{0,3,2,1:T(8,128)S(1)} fusion(bf16[512,4,64,1]{0,2,3,1:T(8,128)(2,1)S(1)} %bitcast.88, f32[4,512,64,8]{1,2,3,0:T(8,128)} %copy-done.1, f32[64,4,8]{0,2,1:T(8,128)S(1)} %max.9, pred[64,512]{1,0:T(8,128)(4,1)S(1)} %broadcast_compare_fusion.3, f32[64,4,8,64]{0,3,2,1:T(8,128)S(1)} %get-tuple-element.354, ...), kind=kOutput, calls=%fused_computation.12.clone.1 | convolution fusion | flops 138805248 | bytes 5554177 | tf_op jit(solution)/shard_map/while/body/eval_jaxpr/tkgr,rkd->tkgd/dot_general | solution.py:113
  73.4 0.6 dynamic_slice.30
  76.2 0.7 fusion.71
  77.0 0.7 fusion.72
  77.7 0.8 fusion.73
  78.5 1.9 %copy-done.1 = f32[4,512,64,8]{1,2,3,0:T(8,128)} copy-done((f32[4,512,64,8]{1,2,3,0:T(8,128)}, f32[4,512,64,8]{1,2,3,0:T(8,128)S(1)}, u32[]{:S(2)}) %copy-start.1) | copy-done | bytes 4194328 | tf_op jit(solution)/shard_map/while
  80.4 1.3 fusion.74
  81.9 3.6 %fusion.76 = f32[64,4,8,64]{0,3,2,1:T(8,128)S(1)} fusion(bf16[512,4,64,1]{0,2,3,1:T(8,128)(2,1)S(1)} %bitcast.88, f32[4,512,64,8]{1,2,3,0:T(8,128)} %copy-done.1, f32[64,4,8]{0,2,1:T(8,128)S(1)} %max.9, pred[64,512]{1,0:T(8,128)(4,1)S(1)} %broadcast_compare_fusion.3, f32[64,4,8,64]{0,3,2,1:T(8,128)S(1)} %get-tuple-element.354, ...), kind=kOutput, calls=%fused_computation.12.clone.1 | convolution fusion | flops 138805248 | bytes 5554177 | tf_op jit(solution)/shard_map/while/body/eval_jaxpr/tkgr,rkd->tkgd/dot_general | solution.py:113
  85.6 0.2 copy.98
  86.8 9.2 %all_gather.14 = bf16[128,2048]{1,0:T(8,128)(2,1)S(1)} all-gather(bf16[64,2048]{1,0:T(8,128)(2,1)S(1)} %copy.98), channel_id=1, replica_groups=mesh['seq'=16,'fsdp'=2] {'fsdp'}, dimensions={0}, use_global_device_ids=true | all-gather | bytes 786432 | tf_op jit(solution)/shard_map/all_gather | solution.py:150
  96.0 2.8 %convolution_convert_fusion.2 = bf16[128,720]{0,1:T(8,128)(2,1)S(1)} fusion(bf16[128,2048]{1,0:T(8,128)(2,1)S(1)} %all_gather.14, bf16[2048,720]{0,1:T(8,128)(2,1)} %all-gather.3.cloned.1.call-done), kind=kOutput, calls=%fused_computation.50 | convolution fusion | flops 377579520 | bytes 3657728 | tf_op jit(solution)/shard_map/dot_general | solution.py:149
  98.8 0.8 copy.87
  99.6 3.4 %all-to-all-start = ((bf16[2,64,720]{2,1,0:T(8,128)(2,1)}), bf16[2,64,720]{2,1,0:T(8,128)(2,1)S(1)}, u32[]{:S(2)}, u32[]{:S(2)}) async-start(bf16[2,64,720]{2,1,0:T(8,128)(2,1)} %bitcast.4), calls=%async_computation | async-start | bytes 393216 | tf_op jit(solution)/shard_map/all_to_all | solution.py:154
  103.1 4.7 %all-to-all-done = bf16[2,64,720]{2,1,0:T(8,128)(2,1)S(1)} async-done(((bf16[2,64,720]{2,1,0:T(8,128)(2,1)}), bf16[2,64,720]{2,1,0:T(8,128)(2,1)S(1)}, u32[]{:S(2)}, u32[]{:S(2)}) %all-to-all-start) | async-done | bytes 184352 | tf_op jit(solution)/shard_map/all_to_all | solution.py:154
  107.9 0.3 copy.94
  108.2 0.3 reshape.357
  108.8 0.3 convolution_convert_fusion.1
  109.1 1.1 reshape_reshape.3
  110.2 3.8 %all-to-all-start.1 = ((bf16[16,12,1440]{2,1,0:T(8,128)(2,1)}), bf16[16,12,1440]{2,1,0:T(8,128)(2,1)S(1)}, u32[]{:S(2)}, u32[]{:S(2)}) async-start(bf16[16,12,1440]{2,1,0:T(8,128)(2,1)} %reshape_reshape.3), calls=%async_computation.1 | async-start | bytes 1572864 | tf_op jit(solution)/shard_map/all_to_all | solution.py:181
  114.2 18.3 %all-to-all-done.1 = bf16[16,12,1440]{2,1,0:T(8,128)(2,1)S(1)} async-done(((bf16[16,12,1440]{2,1,0:T(8,128)(2,1)}), bf16[16,12,1440]{2,1,0:T(8,128)(2,1)S(1)}, u32[]{:S(2)}, u32[]{:S(2)}) %all-to-all-start.1) | async-done | bytes 552992 | tf_op jit(solution)/shard_map/all_to_all | solution.py:181
  132.5 0.3 reshape.350
  132.8 4.3 %fusion.42 = f32[192,1440]{1,0:T(8,128)} fusion(bf16[192,1440]{1,0:T(8,128)(2,1)S(1)} %reshape.350, bf16[1440,1440]{1,0:T(8,128)(2,1)} %param.23), kind=kOutput, calls=%fused_computation.111 | convolution fusion | flops 796262400 | bytes 5806080 | tf_op jit(solution)/shard_map/dot_general | solution.py:57
  137.1 6.0 %convolution_convert_fusion = bf16[192,1440]{1,0:T(8,128)(2,1)S(1)} fusion(bf16[1440,1440]{1,0:T(8,128)(2,1)} %param.25, bf16[192,1440]{1,0:T(8,128)(2,1)S(1)} %reshape.350, bf16[1440,1440]{1,0:T(8,128)(2,1)} %param.24, f32[192,1440]{1,0:T(8,128)} %fusion.42), kind=kOutput, calls=%fused_computation.47 | convolution fusion | flops 1595013120 | bytes 10506240 | tf_op jit(solution)/shard_map/dot_general | solution.py:62
  143.1 1.1 reshape.351
  144.2 5.3 %all-to-all-start.2 = ((bf16[16,12,1440]{2,1,0:T(8,128)(2,1)}), bf16[16,12,1440]{2,1,0:T(8,128)(2,1)S(1)}, u32[]{:S(2)}, u32[]{:S(2)}) async-start(bf16[16,12,1440]{2,1,0:T(8,128)(2,1)} %reshape.351), calls=%async_computation.2 | async-start | bytes 1572864 | tf_op jit(solution)/shard_map/all_to_all | solution.py:187
  150.1 0.2 copy.88
  150.5 17.7 %all-to-all-done.2 = bf16[16,12,1440]{2,1,0:T(8,128)(2,1)S(1)} async-done(((bf16[16,12,1440]{2,1,0:T(8,128)(2,1)}), bf16[16,12,1440]{2,1,0:T(8,128)(2,1)S(1)}, u32[]{:S(2)}, u32[]{:S(2)}) %all-to-all-start.2) | async-done | bytes 552992 | tf_op jit(solution)/shard_map/all_to_all | solution.py:187
  168.2 0.2 reshape.359
  168.4 0.9 gather_fusion
  169.3 0.5 gather.7
  169.8 1.4 multiply_reduce_fusion
  171.2 0.7 fusion.30
  (80 shorter events, 4.4 us)
Async XLA Ops:
  7.2 142.7 %copy-start = (bf16[1440,16]{0,1:T(8,128)(2,1)S(1)}, bf16[1440,16]{0,1:T(8,128)(2,1)}, u32[]{:S(2)}) copy-start(bf16[1440,16]{0,1:T(8,128)(2,1)} %param.22) | copy-start | bytes 138244
  7.2 4.4 %copy-start.5 = (bf16[1,64,256]{2,1,0:T(8,128)(2,1)S(1)}, bf16[1,64,256]{2,1,0:T(8,128)(2,1)}, u32[]{:S(2)}) copy-start(bf16[1,64,256]{2,1,0:T(8,128)(2,1)} %param.17) | copy-start | bytes 98308
  7.2 30.4 %copy-start.10 = (f32[32]{0:T(128)S(1)}, f32[32]{0:T(128)}, u32[]{:S(2)}) copy-start(f32[32]{0:T(128)} %param.19) | copy-start | bytes 388
  7.2 88.8 %all-gather.3.cloned.1.call-start = ((), (), s32[]{:S(2)}) async-start(), calls=%async_computation.3 | async-start | bytes 3133440 | tf_op jit(solution)/shard_map/all_gather | solution.py:148
  11.6 28.9 %copy-start.6 = (bf16[1,64,256]{2,1,0:T(8,128)(2,1)S(1)}, bf16[1,64,256]{2,1,0:T(8,128)(2,1)}, u32[]{:S(2)}) copy-start(bf16[1,64,256]{2,1,0:T(8,128)(2,1)} %param.18) | copy-start | bytes 98308
  11.6 49.7 %copy-start.3 = (f32[64,4,8,64]{0,3,2,1:T(8,128)S(1)}, f32[64,4,8,64]{0,3,2,1:T(8,128)}, u32[]{:S(2)}) copy-start(f32[64,4,8,64]{0,3,2,1:T(8,128)} %custom-call.1) | copy-start | bytes 1572868
  11.6 49.7 %copy-start.7 = (s32[32]{0:T(128)S(1)}, s32[32]{0:T(128)}, u32[]{:S(2)}) copy-start(s32[32]{0:T(128)} %param.27) | copy-start | bytes 388
  61.3 24.5 %copy-start.9 = (bf16[1440]{0:T(1024)(128)(2,1)S(1)}, bf16[1440]{0:T(1024)(128)(2,1)}, u32[]{:S(2)}) copy-start(bf16[1440]{0:T(1024)(128)(2,1)} %param.21) | copy-start | bytes 8644
  61.3 24.6 %copy-start.8 = (s32[1,64,2]{1,2,0:T(2,128)S(1)}, s32[1,64,2]{1,2,0:T(2,128)}, u32[]{:S(2)}) copy-start(s32[1,64,2]{1,2,0:T(2,128)} %param.26) | copy-start | bytes 1540
  66.4 1.9 %copy-start.1 = (f32[4,512,64,8]{1,2,3,0:T(8,128)}, f32[4,512,64,8]{1,2,3,0:T(8,128)S(1)}, u32[]{:S(2)}) copy-start(f32[4,512,64,8]{1,2,3,0:T(8,128)S(1)} %get-tuple-element.334) | copy-start | bytes 12582916 | tf_op jit(solution)/shard_map/while
  78.5 1.9 %copy-start.1 = (f32[4,512,64,8]{1,2,3,0:T(8,128)}, f32[4,512,64,8]{1,2,3,0:T(8,128)S(1)}, u32[]{:S(2)}) copy-start(f32[4,512,64,8]{1,2,3,0:T(8,128)S(1)} %get-tuple-element.334) | copy-start | bytes 12582916 | tf_op jit(solution)/shard_map/while
  85.6 22.9 %copy-start.2 = (bf16[1,64,1440]{2,1,0:T(8,128)(2,1)S(1)}, bf16[1,64,1440]{2,1,0:T(8,128)(2,1)}, u32[]{:S(2)}) copy-start(bf16[1,64,1440]{2,1,0:T(8,128)(2,1)} %param.15) | copy-start | bytes 552964
  99.6 8.2 %all-to-all-start = ((bf16[2,64,720]{2,1,0:T(8,128)(2,1)}), bf16[2,64,720]{2,1,0:T(8,128)(2,1)S(1)}, u32[]{:S(2)}, u32[]{:S(2)}) async-start(bf16[2,64,720]{2,1,0:T(8,128)(2,1)} %bitcast.4), calls=%async_computation | async-start | bytes 393216 | tf_op jit(solution)/shard_map/all_to_all | solution.py:154
  110.2 22.3 %all-to-all-start.1 = ((bf16[16,12,1440]{2,1,0:T(8,128)(2,1)}), bf16[16,12,1440]{2,1,0:T(8,128)(2,1)S(1)}, u32[]{:S(2)}, u32[]{:S(2)}) async-start(bf16[16,12,1440]{2,1,0:T(8,128)(2,1)} %reshape_reshape.3), calls=%async_computation.1 | async-start | bytes 1572864 | tf_op jit(solution)/shard_map/all_to_all | solution.py:181
  144.2 24.0 %all-to-all-start.2 = ((bf16[16,12,1440]{2,1,0:T(8,128)(2,1)}), bf16[16,12,1440]{2,1,0:T(8,128)(2,1)S(1)}, u32[]{:S(2)}, u32[]{:S(2)}) async-start(bf16[16,12,1440]{2,1,0:T(8,128)(2,1)} %reshape.351), calls=%async_computation.2 | async-start | bytes 1572864 | tf_op jit(solution)/shard_map/all_to_all | solution.py:187
  150.5 20.7 %copy-start.4 = (bf16[1,64,1440]{2,1,0:T(8,128)(2,1)}, bf16[1,64,1440]{2,1,0:T(8,128)(2,1)S(1)}, u32[]{:S(2)}) copy-start(bf16[1,64,1440]{2,1,0:T(8,128)(2,1)S(1)} %broadcast_in_dim.128) | copy-start | bytes 552964
Sparse Core Ops, SparseCore 0:
  10.2 51.8 all-gather.2
where the time goes:
time: 180 us; the launch traced here: 179 us
  blocking collectives  55.3 us (31%)
  waiting for transfers between devices  41.3 us (23%)
  matrix products  22.3 us (12%)
  local copies, waits for them, and re-layouts  16 us (9%)
  between operations  14.4 us (8%)
  other arithmetic  12.7 us (7%)
  starting transfers between devices  12.6 us (7%)
  loops' own time  4.08 us (2%)
    all_gather x1, blocking collectives, on_device(): key_piece = lax.all_gather(key_rot, 'seq', axis=0, tiled=True)  25.3 us
    all_gather x1, blocking collectives, on_device(): value_piece = lax.all_gather(values[0], 'seq', axis=0, tiled=True)  20.8 us
    all_to_all x1, waiting for transfers between devices, on_device(): lax.all_to_all(outgoing, 'seq', split_axis=0, concat_axis=0, tiled=True)  18.3 us
    all_to_all x1, waiting for transfers between devices, on_device(): lax.all_to_all(partial_value.reshape(sources, slot_count, D), 'seq', spli...  17.7 us
    all_gather x1, blocking collectives, on_device(): lax.all_gather(attention_rows, 'fsdp', axis=0, tiled=True)  9.25 us
    dot_general x2, matrix products, block_update(): jnp.einsum('tkgr,rkd->tkgd', weights.astype(jnp.bfloat16), value_heads, p...  7.12 us
    dot_general x1, matrix products, expert_block(): jnp.dot(hidden, down_weight, preferred_element_type=jnp.float32)  6.01 us
    all_to_all x1, starting transfers between devices, on_device(): lax.all_to_all(partial_value.reshape(sources, slot_count, D), 'seq', spli...  5.33 us
  transfers between devices with their start and end apart: 4, of which 3 were waited for; matrix products, arithmetic and copies ran while one was open for 14% of the time, Pallas kernels for 0%

commit v1 on v0

v1 whole, which is shorter than its diff:
```python
import functools

import jax
import jax.numpy as jnp
from jax import lax
from jax.experimental import pallas as pl
from jax.experimental.pallas import tpu as pltpu
from jax.sharding import PartitionSpec as P

D = 1440
HEADS = 32
KVH = 4
HD = 64
EXPERTS = 16
TOPK = 2
TOK_DEV = 64
HALF = 32
CAP = 12


rope_base = 150000.0
norm_eps = 1e-05
masked_score = -1e30
block_rows = 512


def lookup(table_values, lookup_index):
    matches = lookup_index[:, None] == jnp.arange(table_values.shape[0], dtype=jnp.int32)[None, :]
    return jnp.sum(jnp.where(matches, table_values[None, :], 0), axis=1)


def positions(span_order, row_index):
    device = row_index // TOK_DEV
    within = row_index % TOK_DEV
    span_index = lookup(span_order, 2 * device + within // HALF)
    return span_index * HALF + within % HALF


def rotate(head_values, where_at):
    half_size = head_values.shape[-1] // 2
    frequency = jnp.exp(-jnp.log(rope_base) * jnp.arange(half_size, dtype=jnp.float32) / half_size)
    angles = where_at.astype(jnp.float32)[:, None] * frequency[None, :]
    cosine = jnp.cos(angles)[:, None, :]
    sine_part = jnp.sin(angles)[:, None, :]
    first_half = head_values[..., :half_size]
    second = head_values[..., half_size:]
    return jnp.concatenate(
        [first_half * cosine - second * sine_part, second * cosine + first_half * sine_part],
        axis=-1,
    )


def slot_of(chosen):
    flattened = chosen.reshape(-1)
    onehot = (flattened[:, None] == jnp.arange(EXPERTS, dtype=jnp.int32)[None, :]).astype(jnp.int32)
    before = jnp.cumsum(onehot, axis=0) - onehot
    return jnp.sum(before * onehot, axis=1).reshape(chosen.shape)


MESH = pl.DeviceIdType.MESH


def remote(source, target, send_sem, recv_sem, **where):
    return pltpu.make_async_remote_copy(
        src_ref=source,
        dst_ref=target,
        send_sem=send_sem,
        recv_sem=recv_sem,
        device_id=where,
        device_id_type=MESH,
    )


def greet(peers):
    barrier = pltpu.get_barrier_semaphore()
    for where in peers:
        pl.semaphore_signal(barrier, inc=1, device_id=where, device_id_type=MESH)
    pl.semaphore_wait(barrier, len(peers))


def gather_plan(block, slots, sems, z_count, z, y, c):
    z_send, z_recv, y_send, y_recv, c_send, c_recv, own_sem = sems

    def slot(zz, yy, cc):
        return (zz * 2 + yy) * 2 + cc

    def z_of(d):
        return lax.rem(z + z_count - d, z_count)

    own = slot(z, y, c)
    to_z = [
        remote(block, slots.at[own], z_send.at[d], z_recv.at[d], seq=slot(lax.rem(z + d, z_count), y, c))
        for d in range(1, z_count)
    ]

    def to_y(d):
        source = block if d == 0 else slots.at[slot(z_of(d), y, c)]
        return remote(source, slots.at[slot(z_of(d), y, c)], y_send.at[d], y_recv.at[d], seq=slot(z, 1 - y, c))

    def to_c(side, d):
        index = slot(z_of(d), y if side == 0 else 1 - y, c)
        source = block if side == 0 and d == 0 else slots.at[index]
        return remote(source, slots.at[index], c_send.at[side, d], c_recv.at[side, d], seq=slot(z, y, 1 - c))

    local = pltpu.make_async_copy(block, slots.at[own], own_sem)
    ys = [to_y(d) for d in range(z_count)]
    cs = [[to_c(side, d) for d in range(z_count)] for side in range(2)]

    def start_z():
        local.start()
        for copy in to_z:
            copy.start()

    def relay(d):
        if d > 0:
            to_z[d - 1].wait_recv()
        ys[d].start()
        cs[0][d].start()

    def relay_across(d):
        ys[d].wait_recv()
        cs[1][d].start()

    def finish():
        for side in range(2):
            for d in range(z_count):
                cs[side][d].wait_recv()
        local.wait()

    def drain():
        for copy in to_z + ys + cs[0] + cs[1]:
            copy.wait_send()

    return start_z, relay, relay_across, finish, drain


def attend_kernel(
    seq_count, fsdp_count,
    q_ref, kv_ref, w_ref, qpos_ref, kpos_ref, sink_ref,
    out_ref,
    kv_all, w_all, bias, rows_all, proj, got,
    kzs, kzr, kys, kyr, kcs, kcr, wzs, wzr, wys, wyr, wcs, wcr, own_sems, as_, ar, ps, pr,
):
    me = lax.axis_index("seq")
    f_me = lax.axis_index("fsdp")
    z_count = seq_count // 4
    z, y, c = me // 4, lax.rem(me // 2, 2), lax.rem(me, 2)
    peers = [{"seq": (lax.rem(z + d, z_count) * 2 + y) * 2 + c} for d in range(1, z_count)]
    peers += [{"seq": (z * 2 + 1 - y) * 2 + c}, {"seq": (z * 2 + y) * 2 + 1 - c}]
    peers += [{"fsdp": lax.rem(f_me + d, fsdp_count)} for d in range(1, fsdp_count)]
    greet(peers)

    kv = gather_plan(kv_ref, kv_all, (kzs, kzr, kys, kyr, kcs, kcr, own_sems.at[0]), z_count, z, y, c)
    w = gather_plan(w_ref, w_all, (wzs, wzr, wys, wyr, wcs, wcr, own_sems.at[1]), z_count, z, y, c)
    kv[0]()
    for d in range(z_count):
        kv[1](d)
    w[0]()
    bias[...] = jnp.where(kpos_ref[...] <= qpos_ref[...], 0.0, masked_score)
    for d in range(z_count):
        kv[2](d)
    w[1](0)
    kv[3]()

    rows, key_count = bias.shape
    group_size = HEADS // KVH
    chunk = 4
    pending = [("z", d) for d in range(1, z_count)] + [("y", d) for d in range(z_count)]
    steps = KVH * (group_size // chunk)
    per_step = -(-len(pending) // steps)

    def send_rows(g):
        return [
            remote(
                rows_all.at[g, f_me], rows_all.at[g, f_me], as_.at[g, d], ar.at[g, d],
                fsdp=lax.rem(f_me + d, fsdp_count),
            )
            for d in range(1, fsdp_count)
        ]

    row_copies = [send_rows(g) for g in range(KVH)]
    for g in range(KVH):
        keys = kv_all[:, :, g * HD:(g + 1) * HD].reshape(key_count, HD)
        vals = kv_all[:, :, (KVH + g) * HD:(KVH + g + 1) * HD].reshape(key_count, HD)
        parts = []
        for part in range(group_size // chunk):
            q = q_ref[g, part * chunk * rows:(part + 1) * chunk * rows, :]
            s = lax.dot_general(q, keys, (((1,), (1,)), ((), ())), preferred_element_type=jnp.float32)
            weights, totals = [], []
            for i in range(chunk):
                sink = sink_ref[0, g * group_size + part * chunk + i]
                one = s[i * rows:(i + 1) * rows, :] + bias[...]
                top = jnp.maximum(jnp.max(one, axis=1, keepdims=True), sink)
                p = jnp.exp(one - top)
                totals.append(jnp.sum(p, axis=1, keepdims=True) + jnp.exp(sink - top))
                weights.append(p.astype(jnp.bfloat16))
            o = jnp.dot(jnp.concatenate(weights, axis=0), vals, preferred_element_type=jnp.float32)
            for i in range(chunk):
                parts.append((o[i * rows:(i + 1) * rows, :] / totals[i]).astype(jnp.bfloat16))
            if part == 0 and g > 0:
                for copy in row_copies[g - 1]:
                    copy.start()
        rows_all[g, pl.ds(f_me, 1)] = jnp.concatenate(parts, axis=1)[None]
    for kind, d in pending:
        w[1](d) if kind == "z" else w[2](d)
    for copy in row_copies[KVH - 1]:
        copy.start()
    w[3]()

    width = group_size * HD
    per = w_ref.shape[0]
    count = width // per
    total = None
    for g in range(KVH):
        for copy in row_copies[g]:
            copy.wait_recv()
        block = w_all[g * count:(g + 1) * count].reshape(width, w_ref.shape[1])
        term = jnp.dot(
            rows_all[g].reshape(fsdp_count * rows, width), block, preferred_element_type=jnp.float32
        )
        total = term if total is None else total + term
    proj[...] = total.astype(jnp.bfloat16).reshape(proj.shape)
    backs = []
    for d in range(1, fsdp_count):
        peer = lax.rem(f_me + d, fsdp_count)
        backs.append(remote(proj.at[peer], got.at[f_me], ps.at[d], pr.at[d], fsdp=peer))
    for copy in backs:
        copy.start()
    got[pl.ds(f_me, 1)] = proj[pl.ds(f_me, 1)]
    kv[4]()
    w[4]()
    for g in range(KVH):
        for copy in row_copies[g]:
            copy.wait_send()
    for copy in backs:
        copy.wait_recv()
    out_ref[...] = got[...]
    for copy in backs:
        copy.wait_send()


def attend(seq_count, fsdp_count, q, kv, w, qpos, kpos, sinks):
    rows = kv.shape[0]
    z_count = seq_count // 4
    dma = pltpu.SemaphoreType.DMA
    vmem = pl.BlockSpec(memory_space=pltpu.VMEM)
    gather_sems = [dma((z_count,))] * 4 + [dma((2, z_count))] * 2
    return pl.pallas_call(
        functools.partial(attend_kernel, seq_count, fsdp_count),
        out_shape=jax.ShapeDtypeStruct((fsdp_count, rows, w.shape[1]), jnp.bfloat16),
        in_specs=[vmem] * 5 + [pl.BlockSpec(memory_space=pltpu.SMEM)],
        out_specs=vmem,
        scratch_shapes=[
            pltpu.VMEM((seq_count,) + kv.shape, jnp.bfloat16),
            pltpu.VMEM((seq_count,) + w.shape, jnp.bfloat16),
            pltpu.VMEM((rows, seq_count * rows), jnp.float32),
            pltpu.VMEM((KVH, fsdp_count, rows, HEADS // KVH * HD), jnp.bfloat16),
            pltpu.VMEM((fsdp_count, rows, w.shape[1]), jnp.bfloat16),
            pltpu.VMEM((fsdp_count, rows, w.shape[1]), jnp.bfloat16),
        ]
        + gather_sems
        + gather_sems
        + [dma((2,)), dma((KVH, fsdp_count)), dma((KVH, fsdp_count)), dma((fsdp_count,)), dma((fsdp_count,))],
        compiler_params=pltpu.CompilerParams(
            collective_id=0, has_side_effects=True, vmem_limit_bytes=60 * 1024 * 1024
        ),
    )(q, kv, w, qpos, kpos, sinks)


def expert_kernel(
    seq_count, copies,
    x_ref, gate_hbm, up_hbm, down_hbm,
    out_ref,
    gate, up, down, arrived, stacked, back, load_sems, xs, xr, bs, br, own_sems,
):
    loads = [
        pltpu.make_async_copy(source, target, load_sems.at[i])
        for i, (source, target) in enumerate(((gate_hbm, gate), (up_hbm, up), (down_hbm, down)))
    ]
    for load in loads:
        load.start()
    me = lax.axis_index("seq")
    greet([{"seq": lax.rem(me + d, seq_count)} for d in range(1, seq_count)])
    sends = []
    for d in range(1, seq_count):
        peer = lax.rem(me + d, seq_count)
        sends.append(remote(x_ref.at[peer // copies], arrived.at[me], xs.at[d], xr.at[d], seq=peer))
    own = pltpu.make_async_copy(x_ref.at[me // copies], arrived.at[me], own_sems.at[0])
    for copy in sends:
        copy.start()
    own.start()
    for copy in sends:
        copy.wait_recv()
    own.wait()
    for i in range(seq_count):
        stacked[i * CAP:(i + 1) * CAP, :] = arrived[i]
    for load in loads:
        load.wait()
    x = stacked[...]
    g = jnp.dot(x, gate[...], preferred_element_type=jnp.float32)
    u = jnp.dot(x, up[...], preferred_element_type=jnp.float32)
    hidden = (g * jax.nn.sigmoid(1.702 * g) * (u + 1.0)).astype(jnp.bfloat16)
    part = jnp.dot(hidden, down[...], preferred_element_type=jnp.float32).astype(jnp.bfloat16)
    for i in range(seq_count):
        back[i] = part[i * CAP:(i + 1) * CAP, :]
    returns = []
    for d in range(1, seq_count):
        peer = lax.rem(me + d, seq_count)
        returns.append(remote(back.at[peer], out_ref.at[me], bs.at[d], br.at[d], seq=peer))
    keep = pltpu.make_async_copy(back.at[me], out_ref.at[me], own_sems.at[1])
    for copy in returns:
        copy.start()
    keep.start()
    for copy in sends:
        copy.wait_send()
    for copy in returns:
        copy.wait_recv()
    keep.wait()
    for copy in returns:
        copy.wait_send()


def run_experts(seq_count, copies, x, gate_weight, up_weight, down_weight):
    dma = pltpu.SemaphoreType.DMA
    vmem = pl.BlockSpec(memory_space=pltpu.VMEM)
    hbm = pl.BlockSpec(memory_space=pl.ANY)
    cap, width = x.shape[1:]
    return pl.pallas_call(
        functools.partial(expert_kernel, seq_count, copies),
        out_shape=jax.ShapeDtypeStruct((seq_count, cap, width), jnp.bfloat16),
        in_specs=[vmem] + [hbm] * 3,
        out_specs=vmem,
        scratch_shapes=[
            pltpu.VMEM(gate_weight.shape, jnp.bfloat16),
            pltpu.VMEM(up_weight.shape, jnp.bfloat16),
            pltpu.VMEM(down_weight.shape, jnp.bfloat16),
            pltpu.VMEM((seq_count, cap, width), jnp.bfloat16),
            pltpu.VMEM((seq_count * cap, width), jnp.bfloat16),
            pltpu.VMEM((seq_count, cap, width), jnp.bfloat16),
            dma((3,)),
            dma((seq_count,)),
            dma((seq_count,)),
            dma((seq_count,)),
            dma((seq_count,)),
            dma((2,)),
        ],
        compiler_params=pltpu.CompilerParams(
            collective_id=1, has_side_effects=True, vmem_limit_bytes=60 * 1024 * 1024
        ),
    )(x, gate_weight, up_weight, down_weight)


def on_device(
    residual,
    queries,
    key_rows,
    values,
    attention_sinks,
    out_weight,
    norm_gain,
    router_weight,
    gate_weight,
    up_weight,
    down_weight,
    routing,
    span_order,
):
    seq_count = lax.axis_size("seq")
    seq_index = lax.axis_index("seq")
    token_count = residual.shape[1]
    group_size = HEADS // KVH
    score_scale = HD ** (-0.5)
    query_at = positions(
        span_order, seq_index * token_count + jnp.arange(token_count, dtype=jnp.int32)
    )
    query_rot = rotate(
        queries[0].astype(jnp.float32).reshape(token_count, HEADS, HD), query_at
    ).astype(jnp.bfloat16)
    query_rot = (query_rot * score_scale).reshape(token_count, KVH, group_size, HD)
    query_rot = query_rot.transpose(1, 2, 0, 3).reshape(KVH, group_size * token_count, HD)
    key_rot = rotate(
        key_rows[0].astype(jnp.float32).reshape(token_count, KVH, HD), query_at
    ).astype(jnp.bfloat16)
    key_rot = key_rot.reshape(token_count, KVH * HD)
    kv = jnp.concatenate([key_rot, values[0]], axis=1)
    key_at = positions(span_order, jnp.arange(seq_count * token_count, dtype=jnp.int32))
    blocks = attend(
        seq_count,
        lax.axis_size("fsdp"),
        query_rot,
        kv,
        out_weight,
        query_at[:, None],
        key_at[None, :],
        attention_sinks[None, :],
    )
    attended = jnp.transpose(blocks, (1, 0, 2)).reshape(token_count, D)
    stream = residual[0].astype(jnp.float32) + attended.astype(jnp.float32)
    normed = (
        stream
        * lax.rsqrt(jnp.mean(stream * stream, axis=-1, keepdims=True) + norm_eps)
        * norm_gain.astype(jnp.float32)
    ).astype(jnp.bfloat16)
    logits = jnp.dot(normed, router_weight, preferred_element_type=jnp.float32)
    chosen = routing[0]
    matches = chosen[:, :, None] == jnp.arange(EXPERTS, dtype=jnp.int32)[None, None, :]
    chosen_logits = jnp.sum(jnp.where(matches, logits[:, None, :], 0.0), axis=-1)
    gates = 1.0 / jnp.sum(jnp.exp(chosen_logits[:, :, None] - chosen_logits[:, None, :]), axis=1)
    slot_index = slot_of(chosen)
    target = chosen * CAP + slot_index
    dispatch_map = jnp.sum(
        (target[None, :, :] == jnp.arange(EXPERTS * CAP, dtype=jnp.int32)[:, None, None]).astype(
            jnp.int32
        ),
        axis=2,
    )
    buffer = jnp.dot(
        dispatch_map.astype(jnp.bfloat16), normed, preferred_element_type=jnp.float32
    ).astype(jnp.bfloat16)
    copies = seq_count // EXPERTS
    returned = run_experts(
        seq_count,
        copies,
        buffer.reshape(EXPERTS, CAP, D),
        gate_weight,
        up_weight,
        down_weight,
    )
    summed = jnp.sum(returned.reshape(EXPERTS, copies, CAP, D).astype(jnp.float32), axis=1).reshape(
        EXPERTS * CAP, D
    )
    chosen_out = jnp.take(summed, target.reshape(-1), axis=0).reshape(token_count, TOPK, D)
    expert_mix = jnp.sum(chosen_out * gates[:, :, None], axis=1)
    layer_output = (stream + expert_mix).astype(jnp.bfloat16)
    return (attended[None], layer_output[None])


def solution(mesh):
    in_specs = (
        P("fsdp", "seq", None),
        P("fsdp", "seq", None),
        P("fsdp", "seq", None),
        P("fsdp", "seq", None),
        P(),
        P("seq", "fsdp"),
        P(),
        P(),
        P(None, "seq"),
        P(None, "seq"),
        P("seq", None),
        P("fsdp", "seq", None),
        P(),
    )
    out_specs = (P("fsdp", "seq", None), P("fsdp", "seq", None))
    return jax.shard_map(
        on_device, mesh=mesh, in_specs=in_specs, out_specs=out_specs, check_vma=False
    )
```

time: 180 us -> 111 us (0.62)
  the two profiles are of different devices: /device:TPU:0 before, /device:TPU:31 now
where the time goes in v1:
time: 111 us
  Pallas kernels  91.2 us (82%)
  local copies, waits for them, and re-layouts  9.04 us (8%)
  other arithmetic  8.82 us (8%)
    pallas_call x1, Pallas kernels, run_experts(): pl.pallas_call(functools.partial(expert_kernel, seq_count, copies), out_s...  48.7 us
    pallas_call x1, Pallas kernels, attend(): pl.pallas_call(functools.partial(attend_kernel, seq_count, fsdp_count), o...  42.5 us

profile of v1, /device:TPU:31, one launch (start us, length us, event | category | flops | bytes accessed | tf_op | source)
XLA Modules:
  0.0 110.6 jit_solution(1742436308555618504)
XLA Ops:
  0.6 0.0 copy-start
  0.7 0.7 select_reduce_fusion.3
  1.5 0.2 multiply_cosine_fusion
  1.7 1.4 %reshape.405 = f32[64,32,64]{2,1,0:T(8,128)S(1)} reshape(bf16[1,64,2048]{2,1,0:T(8,128)(2,1)} %param.14) | data formatting | bytes 786432 | tf_op jit(solution)/shard_map/convert_element_type | solution.py:377
  3.1 0.5 subtract_convert_fusion
  3.6 0.2 copy.41
  3.8 0.2 copy.42
  4.0 1.1 %maximum_multiply_fusion = bf16[64,4,8,64]{3,0,2,1:T(8,128)(2,1)} fusion(bf16[64,4,8,32]{3,0,2,1:T(8,128)(2,1)S(1)} %bitcast.36, bf16[64,4,8,32]{3,0,2,1:T(8,128)(2,1)S(1)} %bitcast.35), kind=kLoop, calls=%fused_computation.5 | loop fusion | flops 786432 | bytes 524288 | tf_op jit(solution)/shard_map/mul | solution.py:379
  5.2 0.1 reshape.406
  5.3 0.2 subtract_convert_fusion.1
  5.5 0.1 pad_maximum_fusion
  5.6 0.1 convert_element_type.82
  5.7 0.6 pad_maximum_fusion.1.kv_ref
  6.3 0.1 copy.43
  6.4 0.6 fusion.6.qpos_ref
  7.1 0.8 copy.44.w_ref
  7.9 0.1 select_reduce_fusion
  8.0 0.6 fusion.17.kpos_ref
  8.6 42.5 %shard_map.140 = bf16[2,64,720]{2,1,0:T(8,128)(2,1)} custom-call(bf16[4,512,64]{2,1,0:T(8,128)(2,1)} %bitcast.34, bf16[64,512]{1,0:T(8,128)(2,1)} %pad_maximum_fusion.1.kv_ref, bf16[128,720]{1,0:T(8,128)(2,1)} %copy.44.w_ref, s32[64,1]{1,0:T(8,128)} %fusion.6.qpos_ref, s32[1,1024]{1,0:T(1,128)} %fusion.17.kpos_ref, f32[1,32]{1,0:T(1,128)} %bitcast.42), custom_call_target="tpu_custom_call" | custom-call | tf_op jit(solution)/shard_map/pallas_call | solution.py:248
  51.1 1.0 bitcast_convert_fusion
  52.0 0.3 copy.51
  52.4 0.3 reshape.408
  52.7 0.2 multiply_reduce_fusion.1
  52.9 0.1 multiply_convert_fusion
  53.0 0.1 copy.46
  53.1 0.1 squeeze.13
  53.2 0.1 fusion.3
  53.3 0.2 reduce_window_sum.11
  53.5 0.2 select_reduce_fusion.1
  53.7 0.1 reshape.401
  53.8 0.1 copy.50
  53.9 0.1 convert_reduce_fusion
  54.0 0.3 convolution_convert_fusion
  54.4 1.1 reshape.402.x_ref
  55.4 48.7 %shard_map.141 = bf16[16,12,1440]{2,1,0:T(8,128)(2,1)} custom-call(bf16[16,12,1440]{2,1,0:T(8,128)(2,1)} %reshape.402.x_ref, bf16[1440,1440]{1,0:T(8,128)(2,1)} %gate_hbm.1, bf16[1440,1440]{1,0:T(8,128)(2,1)} %up_hbm.1, bf16[1440,1440]{1,0:T(8,128)(2,1)} %down_hbm.1), custom_call_target="tpu_custom_call" | custom-call | tf_op jit(solution)/shard_map/pallas_call | solution.py:328
  104.2 1.6 %reshape.410 = f32[192,1440]{1,0:T(8,128)S(1)} reshape(bf16[16,12,1440]{2,1,0:T(8,128)(2,1)} %shard_map.141) | data formatting | bytes 1658880 | tf_op jit(solution)/shard_map/reshape | solution.py:429
  105.8 0.1 mul.238
  106.0 0.9 gather_fusion
  106.8 0.5 gather.7
  107.3 0.1 fusion.31
  107.6 0.1 copy.52
  107.7 0.1 reduce_sum.85
  107.8 0.1 copy.47
  107.9 0.1 copy.48
  108.0 1.4 %multiply_reduce_fusion = f32[64,1440]{1,0:T(8,128)S(1)} fusion(f32[64,2,1440]{2,1,0:T(2,128)S(1)} %gather.7, pred[64,2]{1,0:T(8,128)(4,1)S(1)} %copy.48, f32[64,2]{1,0:T(8,128)S(1)} %copy.52), kind=kLoop, calls=%fused_computation.4 | loop fusion | flops 460800 | bytes 1106560 | tf_op jit(solution)/shard_map/reduce_sum | solution.py:433
  109.4 0.2 copy.45
  109.6 0.2 broadcast_in_dim_reshape.3
  109.8 0.7 fusion.1
  (33 shorter events, 0.2 us)
Async XLA Ops:
  0.6 106.7 %copy-start = (bf16[1440,16]{0,1:T(8,128)(2,1)S(1)}, bf16[1440,16]{0,1:T(8,128)(2,1)}, u32[]{:S(2)}) copy-start(bf16[1440,16]{0,1:T(8,128)(2,1)} %param.20) | copy-start | bytes 138244
  0.6 4.5 %copy-start.5 = (bf16[1,64,256]{2,1,0:T(8,128)(2,1)S(1)}, bf16[1,64,256]{2,1,0:T(8,128)(2,1)}, u32[]{:S(2)}) copy-start(bf16[1,64,256]{2,1,0:T(8,128)(2,1)} %param.15) | copy-start | bytes 98308
  1.7 4.0 %copy-start.6 = (bf16[1,64,256]{2,1,0:T(8,128)(2,1)S(1)}, bf16[1,64,256]{2,1,0:T(8,128)(2,1)}, u32[]{:S(2)}) copy-start(bf16[1,64,256]{2,1,0:T(8,128)(2,1)} %param.16) | copy-start | bytes 98308
  1.7 5.4 %copy-start.4 = (bf16[128,720]{0,1:T(8,128)(2,1)S(1)}, bf16[128,720]{0,1:T(8,128)(2,1)}, u32[]{:S(2)}) copy-start(bf16[128,720]{0,1:T(8,128)(2,1)} %param.18) | copy-start | bytes 552964
  3.1 4.8 %copy-start.9 = (s32[32]{0:T(128)S(1)}, s32[32]{0:T(128)}, u32[]{:S(2)}) copy-start(s32[32]{0:T(128)} %param.25) | copy-start | bytes 388
  3.6 49.1 %copy-start.2 = (bf16[1,64,1440]{2,1,0:T(8,128)(2,1)S(1)}, bf16[1,64,1440]{2,1,0:T(8,128)(2,1)}, u32[]{:S(2)}) copy-start(bf16[1,64,1440]{2,1,0:T(8,128)(2,1)} %param.13) | copy-start | bytes 552964
  3.6 49.3 %copy-start.8 = (bf16[1440]{0:T(1024)(128)(2,1)S(1)}, bf16[1440]{0:T(1024)(128)(2,1)}, u32[]{:S(2)}) copy-start(bf16[1440]{0:T(1024)(128)(2,1)} %param.19) | copy-start | bytes 8644
  3.8 49.2 %copy-start.7 = (s32[1,64,2]{1,2,0:T(2,128)S(1)}, s32[1,64,2]{1,2,0:T(2,128)}, u32[]{:S(2)}) copy-start(s32[1,64,2]{1,2,0:T(2,128)} %param.24) | copy-start | bytes 1540
  106.0 3.5 %copy-start.1 = (bf16[2,64,720]{2,1,0:T(8,128)(2,1)S(1)}, bf16[2,64,720]{2,1,0:T(8,128)(2,1)}, u32[]{:S(2)}) copy-start(bf16[2,64,720]{2,1,0:T(8,128)(2,1)} %shard_map.140) | copy-start | bytes 552964
  109.8 0.8 copy-start.3

commit v2 on v1

v2 whole, which is shorter than its diff:
```python
import functools

import jax
import jax.numpy as jnp
from jax import lax
from jax.experimental import pallas as pl
from jax.experimental.pallas import tpu as pltpu
from jax.sharding import PartitionSpec as P

D = 1440
HEADS = 32
KVH = 4
HD = 64
EXPERTS = 16
TOPK = 2
TOK_DEV = 64
HALF = 32
CAP = 12


rope_base = 150000.0
norm_eps = 1e-05
masked_score = -1e30


MESH = pl.DeviceIdType.MESH


def remote(source, target, send_sem, recv_sem, **where):
    return pltpu.make_async_remote_copy(
        src_ref=source,
        dst_ref=target,
        send_sem=send_sem,
        recv_sem=recv_sem,
        device_id=where,
        device_id_type=MESH,
    )


def greet(peers):
    barrier = pltpu.get_barrier_semaphore()
    for where in peers:
        pl.semaphore_signal(barrier, inc=1, device_id=where, device_id_type=MESH)
    pl.semaphore_wait(barrier, len(peers))


def gather_plan(block, slots, sems, z_count, z, y, c):
    z_send, z_recv, y_send, y_recv, c_send, c_recv, own_sem = sems

    def slot(zz, yy, cc):
        return (zz * 2 + yy) * 2 + cc

    def z_of(d):
        return lax.rem(z + z_count - d, z_count)

    own = slot(z, y, c)
    to_z = [
        remote(block, slots.at[own], z_send.at[d], z_recv.at[d], seq=slot(lax.rem(z + d, z_count), y, c))
        for d in range(1, z_count)
    ]

    def to_y(d):
        source = block if d == 0 else slots.at[slot(z_of(d), y, c)]
        return remote(source, slots.at[slot(z_of(d), y, c)], y_send.at[d], y_recv.at[d], seq=slot(z, 1 - y, c))

    def to_c(side, d):
        index = slot(z_of(d), y if side == 0 else 1 - y, c)
        source = block if side == 0 and d == 0 else slots.at[index]
        return remote(source, slots.at[index], c_send.at[side, d], c_recv.at[side, d], seq=slot(z, y, 1 - c))

    local = pltpu.make_async_copy(block, slots.at[own], own_sem)
    ys = [to_y(d) for d in range(z_count)]
    cs = [[to_c(side, d) for d in range(z_count)] for side in range(2)]

    def start_z():
        local.start()
        for copy in to_z:
            copy.start()

    def relay(d):
        if d > 0:
            to_z[d - 1].wait_recv()
        ys[d].start()
        cs[0][d].start()

    def relay_across(d):
        ys[d].wait_recv()
        cs[1][d].start()

    def finish():
        for side in range(2):
            for d in range(z_count):
                cs[side][d].wait_recv()
        local.wait()

    def drain():
        for copy in to_z + ys + cs[0] + cs[1]:
            copy.wait_send()

    return start_z, relay, relay_across, finish, drain


def layer_kernel(
    seq_count, fsdp_count,
    sink_ref, span_ref, gain_ref, routing_ref,
    res_hbm, q_hbm, k_hbm, v_hbm, w_hbm, router_hbm, gate_hbm, up_hbm, down_hbm,
    attended_ref, layer_ref,
    res, q_raw, k_raw, v_raw, router, gate, up, down,
    kv_own, kv_all, w_own, w_all, q_rot, bias, rows_all, proj, got,
    x_out, arrived, stacked, back, returned, restacked,
    load_sems,
    kzs, kzr, kys, kyr, kcs, kcr, wzs, wzr, wys, wyr, wcs, wcr, own_sems, as_, ar, ps, pr,
    xs, xr, bs, br,
):
    sources = (k_hbm, v_hbm, w_hbm, q_hbm, res_hbm, router_hbm, gate_hbm, up_hbm, down_hbm)
    targets = (k_raw, v_raw, w_own, q_raw, res, router, gate, up, down)
    loads = [
        pltpu.make_async_copy(a, b, load_sems.at[i]) for i, (a, b) in enumerate(zip(sources, targets))
    ]
    for load in loads[:6]:
        load.start()

    me = lax.axis_index("seq")
    f_me = lax.axis_index("fsdp")
    z_count = seq_count // 4
    z, y, c = me // 4, lax.rem(me // 2, 2), lax.rem(me, 2)
    rows, key_count = bias.shape
    group_size = HEADS // KVH
    copies = seq_count // EXPERTS

    def spot(row):
        return jnp.where(row < HALF, span_ref[0, 2 * me], span_ref[0, 2 * me + 1]) * HALF + row % HALF

    lane = lax.broadcasted_iota(jnp.int32, (rows, 2 * HD), 1)
    place = spot(lax.broadcasted_iota(jnp.int32, (rows, 2 * HD), 0)).astype(jnp.float32)
    half = HD // 2
    frequency = jnp.exp(-jnp.log(rope_base) * (lane % half).astype(jnp.float32) / half)
    angles = place * frequency
    low = (lane % HD) < half
    cosine = jnp.cos(angles)
    sine = jnp.where(low, -jnp.sin(angles), jnp.sin(angles))

    def rotated(pair):
        x = pair.astype(jnp.float32)
        swapped = jnp.where(low, pltpu.roll(x, 2 * HD - half, 1), pltpu.roll(x, half, 1))
        return (x * cosine + swapped * sine).astype(jnp.bfloat16)

    loads[0].wait()
    loads[1].wait()
    for i in range(KVH // 2):
        kv_own[:, i * 2 * HD:(i + 1) * 2 * HD] = rotated(k_raw[:, i * 2 * HD:(i + 1) * 2 * HD])
    kv_own[:, KVH * HD:] = v_raw[...]

    def peer_of(side, dz, cc, sign=1):
        zz = lax.rem(z + dz, z_count) if sign > 0 else lax.rem(z + z_count - dz, z_count)
        return (zz * 2 + (1 - y if side else y)) * 2 + (1 - c if cc else c)

    relative = [(side, dz, cc) for side in range(2) for dz in range(z_count) for cc in range(2)]
    peers = [{"seq": peer_of(*r)} for r in relative[1:]]
    peers += [{"fsdp": lax.rem(f_me + d, fsdp_count)} for d in range(1, fsdp_count)]
    greet(peers)

    kv = gather_plan(kv_own, kv_all, (kzs, kzr, kys, kyr, kcs, kcr, own_sems.at[0]), z_count, z, y, c)
    w = gather_plan(w_own, w_all, (wzs, wzr, wys, wyr, wcs, wcr, own_sems.at[1]), z_count, z, y, c)
    kv[0]()
    kv[1](0)
    loads[2].wait()
    w[0]()
    loads[3].wait()
    for i in range(HEADS // 2):
        pair = rotated(q_raw[:, i * 2 * HD:(i + 1) * 2 * HD]) * jnp.bfloat16(HD ** -0.5)
        g, inside = (2 * i) // group_size, (2 * i) % group_size
        q_rot[g, inside * rows:(inside + 1) * rows, :] = pair[:, :HD]
        q_rot[g, (inside + 1) * rows:(inside + 2) * rows, :] = pair[:, HD:]
    key_row = lax.broadcasted_iota(jnp.int32, (1, key_count), 1)
    span_of_key = jnp.zeros((1, key_count), jnp.int32)
    for i in range(span_ref.shape[1]):
        span_of_key = jnp.where(key_row // HALF == i, span_ref[0, i], span_of_key)
    key_at = span_of_key * HALF + key_row % HALF
    query_at = spot(lax.broadcasted_iota(jnp.int32, (rows, 1), 0))
    bias[...] = jnp.where(key_at <= query_at, 0.0, masked_score)

    chosen = routing_ref[...]
    expert_lane = lax.broadcasted_iota(jnp.int32, (rows, EXPERTS), 1)
    picks = [chosen[:, j:j + 1] == expert_lane for j in range(TOPK)]
    named = sum(p.astype(jnp.float32) for p in picks)
    earlier = lax.broadcasted_iota(jnp.int32, (rows, rows), 1) < lax.broadcasted_iota(
        jnp.int32, (rows, rows), 0
    )
    before = jnp.dot(earlier.astype(jnp.float32), named, preferred_element_type=jnp.float32)
    slots = [
        jnp.sum(jnp.where(p, before, 0.0), axis=1, keepdims=True).astype(jnp.int32) for p in picks
    ]

    for d in range(1, z_count):
        kv[1](d)
    for d in range(z_count):
        kv[2](d)
    w[1](0)
    for load in loads[6:]:
        load.start()
    kv[3]()

    chunk = 4

    def send_rows(g):
        return [
            remote(
                rows_all.at[g, f_me], rows_all.at[g, f_me], as_.at[g, d], ar.at[g, d],
                fsdp=lax.rem(f_me + d, fsdp_count),
            )
            for d in range(1, fsdp_count)
        ]

    row_copies = [send_rows(g) for g in range(KVH)]
    relayed = 1
    for g in range(KVH):
        keys = kv_all[:, :, g * HD:(g + 1) * HD].reshape(key_count, HD)
        vals = kv_all[:, :, (KVH + g) * HD:(KVH + g + 1) * HD].reshape(key_count, HD)
        parts = []
        for part in range(group_size // chunk):
            q = q_rot[g, part * chunk * rows:(part + 1) * chunk * rows, :]
            s = lax.dot_general(q, keys, (((1,), (1,)), ((), ())), preferred_element_type=jnp.float32)
            weights, totals = [], []
            for i in range(chunk):
                sink = sink_ref[0, g * group_size + part * chunk + i]
                one = s[i * rows:(i + 1) * rows, :] + bias[...]
                top = jnp.maximum(jnp.max(one, axis=1, keepdims=True), sink)
                p = jnp.exp(one - top)
                totals.append(jnp.sum(p, axis=1, keepdims=True) + jnp.exp(sink - top))
                weights.append(p.astype(jnp.bfloat16))
            o = jnp.dot(jnp.concatenate(weights, axis=0), vals, preferred_element_type=jnp.float32)
            for i in range(chunk):
                parts.append((o[i * rows:(i + 1) * rows, :] / totals[i]).astype(jnp.bfloat16))
            if part == 0 and g > 0:
                for copy in row_copies[g - 1]:
                    copy.start()
        rows_all[g, pl.ds(f_me, 1)] = jnp.concatenate(parts, axis=1)[None]
        while relayed < z_count and relayed * KVH <= (g + 1) * z_count - KVH:
            w[1](relayed)
            relayed += 1
    for d in range(relayed, z_count):
        w[1](d)
    for copy in row_copies[KVH - 1]:
        copy.start()
    for d in range(z_count):
        w[2](d)
    loads[4].wait()
    loads[5].wait()
    w[3]()

    width = group_size * HD
    count = width // w_own.shape[0]
    total = None
    for g in range(KVH):
        for copy in row_copies[g]:
            copy.wait_recv()
        block = w_all[g * count:(g + 1) * count].reshape(width, w_own.shape[1])
        term = jnp.dot(
            rows_all[g].reshape(fsdp_count * rows, width), block, preferred_element_type=jnp.float32
        )
        total = term if total is None else total + term
    proj[...] = total.astype(jnp.bfloat16).reshape(proj.shape)
    backs = []
    for d in range(1, fsdp_count):
        peer = lax.rem(f_me + d, fsdp_count)
        backs.append(remote(proj.at[peer], got.at[f_me], ps.at[d], pr.at[d], fsdp=peer))
    for copy in backs:
        copy.start()
    got[pl.ds(f_me, 1)] = proj[pl.ds(f_me, 1)]
    kv[4]()
    w[4]()
    for g in range(KVH):
        for copy in row_copies[g]:
            copy.wait_send()
    for copy in backs:
        copy.wait_recv()
    columns = w_own.shape[1]
    for f in range(fsdp_count):
        attended_ref[:, f * columns:(f + 1) * columns] = got[f]
    for copy in backs:
        copy.wait_send()

    stream = res[...].astype(jnp.float32) + attended_ref[...].astype(jnp.float32)
    normed = (
        stream
        * lax.rsqrt(jnp.mean(stream * stream, axis=-1, keepdims=True) + norm_eps)
        * gain_ref[...].astype(jnp.float32)
    ).astype(jnp.bfloat16)
    place_lane = lax.broadcasted_iota(jnp.int32, (rows, EXPERTS * CAP), 1)
    dispatch = sum(
        (place_lane == chosen[:, j:j + 1] * CAP + slots[j]).astype(jnp.float32) for j in range(TOPK)
    ).astype(jnp.bfloat16)
    buffer = lax.dot_general(
        dispatch, normed, (((0,), (0,)), ((), ())), preferred_element_type=jnp.float32
    ).astype(jnp.bfloat16)
    for e in range(EXPERTS):
        x_out[e] = buffer[e * CAP:(e + 1) * CAP, :]

    sends, returns = {}, {}
    for r, rel in enumerate(relative[1:], 1):
        to, source = peer_of(*rel), peer_of(*rel, sign=-1)
        sends[r] = remote(x_out.at[to // copies], arrived.at[r], xs.at[r], xr.at[r], seq=to)
        returns[r] = remote(back.at[r], returned.at[me], bs.at[r], br.at[r], seq=source)
    own = pltpu.make_async_copy(x_out.at[me // copies], arrived.at[0], own_sems.at[2])
    keep = pltpu.make_async_copy(back.at[0], returned.at[me], own_sems.at[3])
    for copy in sends.values():
        copy.start()
    own.start()

    logits = jnp.dot(normed, router[...], preferred_element_type=jnp.float32)
    told = [jnp.sum(jnp.where(p, logits, 0.0), axis=1, keepdims=True) for p in picks]
    gates = [1.0 / sum(jnp.exp(t - told[j]) for t in told) for j in range(TOPK)]
    slot_lane = lax.broadcasted_iota(jnp.int32, (rows, seq_count * CAP), 1)
    mixing = sum(
        jnp.where(
            (slot_lane // (CAP * copies) == chosen[:, j:j + 1]) & (slot_lane % CAP == slots[j]),
            gates[j],
            0.0,
        )
        for j in range(TOPK)
    )
    coarse = mixing.astype(jnp.bfloat16)
    fine = (mixing - coarse.astype(jnp.float32)).astype(jnp.bfloat16)

    for load in loads[6:]:
        load.wait()
    per_side = len(relative) // 2
    for side in range(2):
        for i in range(per_side):
            r = side * per_side + i
            sends[r].wait_recv() if r > 0 else own.wait()
            stacked[i * CAP:(i + 1) * CAP, :] = arrived[r]
        x = stacked[...]
        g = jnp.dot(x, gate[...], preferred_element_type=jnp.float32)
        u = jnp.dot(x, up[...], preferred_element_type=jnp.float32)
        hidden = (g * jax.nn.sigmoid(1.702 * g) * (u + 1.0)).astype(jnp.bfloat16)
        part = jnp.dot(hidden, down[...], preferred_element_type=jnp.float32).astype(jnp.bfloat16)
        for i in range(per_side):
            back[side * per_side + i] = part[i * CAP:(i + 1) * CAP, :]
        for i in range(per_side):
            r = side * per_side + i
            returns[r].start() if r > 0 else keep.start()
    for copy in sends.values():
        copy.wait_send()
    for copy in returns.values():
        copy.wait_recv()
    keep.wait()
    for i in range(seq_count):
        restacked[i * CAP:(i + 1) * CAP, :] = returned[i]
    outs = restacked[...]
    mixed = jnp.dot(coarse, outs, preferred_element_type=jnp.float32) + jnp.dot(
        fine, outs, preferred_element_type=jnp.float32
    )
    layer_ref[...] = (
        res[...].astype(jnp.float32) + attended_ref[...].astype(jnp.float32) + mixed
    ).astype(jnp.bfloat16)
    for copy in returns.values():
        copy.wait_send()


def on_device(
    residual,
    queries,
    key_rows,
    values,
    attention_sinks,
    out_weight,
    norm_gain,
    router_weight,
    gate_weight,
    up_weight,
    down_weight,
    routing,
    span_order,
):
    seq_count = lax.axis_size("seq")
    fsdp_count = lax.axis_size("fsdp")
    z_count = seq_count // 4
    rows = residual.shape[1]
    dma = pltpu.SemaphoreType.DMA
    vmem = pl.BlockSpec(memory_space=pltpu.VMEM)
    smem = pl.BlockSpec(memory_space=pltpu.SMEM)
    hbm = pl.BlockSpec(memory_space=pl.ANY)
    gather_sems = [dma((z_count,))] * 4 + [dma((2, z_count))] * 2

    def held(*shape):
        return pltpu.VMEM(shape, jnp.bfloat16)

    kv_width = 2 * KVH * HD
    w_rows, columns = out_weight.shape
    attended, layer_output = pl.pallas_call(
        functools.partial(layer_kernel, seq_count, fsdp_count),
        out_shape=[jax.ShapeDtypeStruct((rows, D), jnp.bfloat16)] * 2,
        in_specs=[smem, smem, vmem, vmem] + [hbm] * 9,
        out_specs=[vmem, vmem],
        scratch_shapes=[
            held(rows, D),
            held(rows, HEADS * HD),
            held(rows, KVH * HD),
            held(rows, KVH * HD),
            held(*router_weight.shape),
            held(*gate_weight.shape),
            held(*up_weight.shape),
            held(*down_weight.shape),
            held(rows, kv_width),
            held(seq_count, rows, kv_width),
            held(w_rows, columns),
            held(seq_count, w_rows, columns),
            held(KVH, HEADS // KVH * rows, HD),
            pltpu.VMEM((rows, seq_count * rows), jnp.float32),
            held(KVH, fsdp_count, rows, HEADS // KVH * HD),
            held(fsdp_count, rows, columns),
            held(fsdp_count, rows, columns),
            held(EXPERTS, CAP, D),
            held(seq_count, CAP, D),
            held(seq_count // 2 * CAP, D),
            held(seq_count, CAP, D),
            held(seq_count, CAP, D),
            held(seq_count * CAP, D),
            dma((9,)),
        ]
        + gather_sems
        + gather_sems
        + [dma((4,)), dma((KVH, fsdp_count)), dma((KVH, fsdp_count)), dma((fsdp_count,)), dma((fsdp_count,))]
        + [dma((seq_count,))] * 4,
        compiler_params=pltpu.CompilerParams(
            collective_id=0, has_side_effects=True, vmem_limit_bytes=60 * 1024 * 1024
        ),
    )(
        attention_sinks[None, :],
        span_order[None, :],
        norm_gain[None, :],
        routing[0],
        residual[0],
        queries[0],
        key_rows[0],
        values[0],
        out_weight,
        router_weight,
        gate_weight,
        up_weight,
        down_weight,
    )
    return (attended[None], layer_output[None])


def solution(mesh):
    in_specs = (
        P("fsdp", "seq", None),
        P("fsdp", "seq", None),
        P("fsdp", "seq", None),
        P("fsdp", "seq", None),
        P(),
        P("seq", "fsdp"),
        P(),
        P(),
        P(None, "seq"),
        P(None, "seq"),
        P("seq", None),
        P("fsdp", "seq", None),
        P(),
    )
    out_specs = (P("fsdp", "seq", None), P("fsdp", "seq", None))
    return jax.shard_map(
        on_device, mesh=mesh, in_specs=in_specs, out_specs=out_specs, check_vma=False
    )
```

time: 111 us -> 104 us (0.937)
  the two profiles are of different devices: /device:TPU:31 before, /device:TPU:0 now
where the time goes in v2:
time: 104 us
  Pallas kernels  94 us (90%)
  local copies, waits for them, and re-layouts  9.34 us (9%)
    pallas_call x1, Pallas kernels, on_device(): pl.pallas_call(functools.partial(layer_kernel, seq_count, fsdp_count), ou...  94 us
    unnamed x4, local copies, waits for them, and re-layouts  6.68 us

profile of v2, /device:TPU:0, one launch (start us, length us, event | category | flops | bytes accessed | tf_op | source)
XLA Modules:
  0.0 104.0 jit_solution(1987266019710095796)
XLA Ops:
  0.6 1.3 %broadcast_in_dim.17.gain_ref = bf16[1,1440]{1,0:T(2,128)(2,1)} reshape(bf16[1440]{0:T(1024)(128)(2,1)} %param.19) | data formatting | bytes 5760 | tf_op jit(solution)/shard_map/broadcast_in_dim | solution.py:433
  1.9 1.4 %copy.15.routing_ref = s32[64,2]{1,0:T(8,128)} copy(s32[64,2]{0,1:T(2,128)} %bitcast.15) | data formatting | bytes 1024 | tf_op jit(solution)/shard_map/squeeze | solution.py:434
  3.3 1.7 %copy.16.w_hbm = bf16[128,720]{1,0:T(8,128)(2,1)} copy(bf16[128,720]{0,1:T(8,128)(2,1)} %param.18) | data formatting | bytes 368640 | tf_op args[5]
  5.0 1.7 %copy.17.router_hbm = bf16[1440,16]{1,0:T(8,128)(2,1)} copy(bf16[1440,16]{0,1:T(8,128)(2,1)} %param.20) | data formatting | bytes 92160 | tf_op args[7]
  6.7 94.0 %shard_map.140 = (bf16[64,1440]{1,0:T(8,128)(2,1)}, bf16[64,1440]{1,0:T(8,128)(2,1)}) custom-call(f32[1,32]{1,0:T(1,128)} %bitcast.16, s32[1,32]{1,0:T(1,128)} %bitcast.17, bf16[1,1440]{1,0:T(2,128)(2,1)} %broadcast_in_dim.17.gain_ref, s32[64,2]{1,0:T(8,128)} %copy.15.routing_ref, bf16[64,1440]{1,0:T(8,128)(2,1)} %bitcast.10, bf16[64,2048]{1,0:T(8,128)(2,1)} %bitcast.9, ...), custom_call_target="tpu_custom_call" | custom-call | tf_op jit(solution)/shard_map/pallas_call | solution.py:392
  100.7 1.6 %copy.20 = bf16[1,64,1440]{2,1,0:T(8,128)(2,1)} copy(bf16[1,64,1440]{2,1,0:T(8,128)(2,1)} %bitcast.12) | data formatting | bytes 368640
  102.4 1.6 %copy.21 = bf16[1,64,1440]{2,1,0:T(8,128)(2,1)} copy(bf16[1,64,1440]{2,1,0:T(8,128)(2,1)} %bitcast.11) | data formatting | bytes 368640
